TPU v7x, 128 devices: a whole 4x4x4 slice. The times are simulated.
128 devices in a mesh: seq: 32 (over z, x, core), rep: 4 (over y).
Axes of the slice: x: 4, y: 4, z: 4, core: 2. Of those that a mesh axis runs over, the one named last changes fastest.
Arguments:
- tokens: bfloat16 [16384, 2304], P(('rep', 'seq')), parts along dimension 0, may hold values from -6 to 6
- qkv_weight: bfloat16 [2304, 6144], P(None, 'seq'), may hold values from -0.125 to 0.125
- conv_weight: float32 [4, 6144], replicated, may hold values from -3 to 3
- decay_down: bfloat16 [2304, 128], replicated, may hold values from -0.125 to 0.125
- decay_up: bfloat16 [128, 2048], replicated, may hold values from -0.5 to 0.5
- decay_rate: float32 [2048], replicated, may hold values from 0.00024414062 to 0.1
- beta_weight: bfloat16 [2304, 16], replicated, may hold values from -0.125 to 0.125
- beta_scale: float32 [16], replicated, may hold values from 0.03125 to 1
- gate_down: bfloat16 [2304, 128], replicated, may hold values from -0.125 to 0.125
- gate_up: bfloat16 [128, 2048], replicated, may hold values from -0.5 to 0.5
- norm_gain: float32 [128], replicated, may hold values from 0.1 to 1.9
Outputs:
- attended: bfloat16 [16384, 2048], P(('rep', 'seq')), parts along dimension 0
There are 4 independent parts, one for each index of `rep`. A program takes and returns all parts, laid end to end along the dimension named above; an argument that names none is the same for every part. Nothing has to cross between parts.
All inputs are finite; a program needn't handle non-finite values.
Results may differ from a plain program's by a relative error of at most 0.0054.
Values may be sent and summed in bfloat16 or wider, within the bound.
No kernel may reach another device: no remote copies, remote signals or barrier semaphores. Data moves between devices by JAX's collectives and lax.ppermute only.
A program may use at most 192 MiB of HBM per device.

v0:
```python
import jax
import jax.numpy as jnp
from jax import lax
from jax.sharding import PartitionSpec as P

H = 16
DK = 128
CONV = 4
BLOCK = 64
precise = lax.Precision.HIGHEST


def from_behind(block, axis, distance):
    devices = range(lax.axis_size(axis))
    route = [(i - distance, i) for i in devices if i - distance in devices]
    return lax.ppermute(block, axis, route)


def carried_in(x, axis, combine, identity):
    devices, mine = (lax.axis_size(axis), lax.axis_index(axis))
    everything = jax.tree.map(lambda part: lax.all_gather(part, axis), x)
    start = jax.tree.map(
        lambda part, zero: jnp.broadcast_to(jnp.asarray(zero, part.dtype), part.shape), x, identity
    )

    def lap(k, before):
        reached = k < mine
        new = combine(before, jax.tree.map(lambda part: part[k], everything))
        return jax.tree.map(lambda a, b: jnp.where(reached, a, b), new, before)

    return lax.fori_loop(0, devices, lap, start)


def unit_rows(vector):
    return vector * lax.rsqrt(jnp.sum(vector * vector, axis=-1, keepdims=True) + 1e-06)


def features(padded, count, conv_weight):
    combined = conv_weight[0] * padded[0:count].astype(jnp.float32)
    for offset in range(1, CONV):
        combined = combined + conv_weight[offset] * padded[offset : offset + count].astype(
            jnp.float32
        )
    active = jax.nn.silu(combined).reshape(count, 3, H, DK)
    query = unit_rows(active[:, 0]) * DK ** (-0.5)
    keys = unit_rows(active[:, 1])
    values = active[:, 2]
    return (query, keys, values)


def gates(tokens, decay_down, decay_up, decay_rate, beta_weight, beta_scale, gate_down, gate_up):
    beta = beta_scale * jax.nn.sigmoid(
        jnp.dot(tokens, beta_weight, preferred_element_type=jnp.float32)
    )
    decay_low = jnp.dot(tokens, decay_down, preferred_element_type=jnp.float32).astype(jnp.bfloat16)
    logdec = -decay_rate * jax.nn.sigmoid(
        jnp.dot(decay_low, decay_up, preferred_element_type=jnp.float32)
    )
    gate_low = jnp.dot(tokens, gate_down, preferred_element_type=jnp.float32).astype(jnp.bfloat16)
    gate_value = jax.nn.sigmoid(jnp.dot(gate_low, gate_up, preferred_element_type=jnp.float32))
    return (beta, logdec, gate_value)


def to_blocks(array, count):
    return array.reshape(count // BLOCK, BLOCK, H, array.shape[-1]).transpose(0, 2, 1, 3)


def block_terms(query, keys, values, beta, logdec):
    log_sum = jnp.cumsum(logdec, axis=2)
    grow = jnp.exp(log_sum)
    keys_up = keys * grow
    keys_down = keys * jnp.exp(-log_sum)
    query_up = query * grow
    keys_end = keys * jnp.exp(log_sum[:, :, -1:, :] - log_sum)
    length = query.shape[2]
    rows = lax.broadcasted_iota(jnp.int32, (length, length), 0)
    columns = lax.broadcasted_iota(jnp.int32, (length, length), 1)
    scores = jnp.einsum("nhic,nhjc->nhij", keys_up, keys_down, precision=precise) * beta[..., None]
    system = jnp.where(rows > columns, scores, 0.0) + jnp.eye(length, dtype=jnp.float32)
    right_side = jnp.concatenate([values, keys_up], axis=-1) * beta[..., None]
    solved = jax.scipy.linalg.solve_triangular(system, right_side, lower=True, unit_diagonal=True)
    values_w = solved[..., :DK]
    keys_w = solved[..., DK:]
    attend = jnp.where(
        rows >= columns, jnp.einsum("nhic,nhjc->nhij", query_up, keys_down, precision=precise), 0.0
    )
    decay_end = jnp.exp(log_sum[:, :, -1, :])
    return (query_up, keys_end, values_w, keys_w, attend, decay_end)


def advance(state, inputs):
    query_up, keys_end, values_w, keys_w, attend, decay_end = inputs
    update = values_w - jnp.einsum("hcd,hde->hce", keys_w, state, precision=precise)
    output = jnp.einsum("hcd,hde->hce", query_up, state, precision=precise)
    output = output + jnp.einsum("hij,hje->hie", attend, update, precision=precise)
    state = decay_end[..., None] * state + jnp.einsum(
        "hcd,hce->hde", keys_end, update, precision=precise
    )
    return (state, output)


def matmul(left, right):
    return jnp.einsum("...de,...ef->...df", left, right, precision=precise)


def fold_block(carry, inputs):
    matrix, offset = carry
    keys_end, keys_w, values_w, decay_end = inputs
    eye_block = jnp.eye(DK, dtype=jnp.float32)
    block_matrix = decay_end[..., None] * eye_block - jnp.einsum(
        "hcd,hce->hde", keys_end, keys_w, precision=precise
    )
    block_offset = jnp.einsum("hcd,hce->hde", keys_end, values_w, precision=precise)
    return ((matmul(block_matrix, matrix), matmul(block_matrix, offset) + block_offset), None)


def join_pairs(first, second):
    return (matmul(second[0], first[0]), matmul(second[0], first[1]) + second[1])


def finish(core, gate_value, norm_gain, count):
    scaled = core * lax.rsqrt(jnp.mean(core * core, axis=-1, keepdims=True) + 1e-06) * norm_gain
    return (scaled.reshape(count, H * DK) * gate_value).astype(jnp.bfloat16)


def per_device(
    tokens,
    qkv_weight,
    conv_weight,
    decay_down,
    decay_up,
    decay_rate,
    beta_weight,
    beta_scale,
    gate_down,
    gate_up,
    norm_gain,
):
    count = tokens.shape[0]
    mixed = jnp.dot(
        tokens,
        lax.all_gather(qkv_weight, "seq", axis=1, tiled=True),
        preferred_element_type=jnp.float32,
    ).astype(jnp.bfloat16)
    earlier = from_behind(mixed[count - (CONV - 1) :], "seq", 1)
    padded = jnp.concatenate([earlier, mixed], axis=0)
    query, keys, values = features(padded, count, conv_weight)
    beta, logdec, gate_value = gates(
        tokens, decay_down, decay_up, decay_rate, beta_weight, beta_scale, gate_down, gate_up
    )
    beta_blocks = beta.reshape(count // BLOCK, BLOCK, H).transpose(0, 2, 1)
    terms = block_terms(
        to_blocks(query, count),
        to_blocks(keys, count),
        to_blocks(values, count),
        beta_blocks,
        to_blocks(logdec.reshape(count, H, DK), count),
    )
    query_up, keys_end, values_w, keys_w, attend, decay_end = terms
    identity = jnp.broadcast_to(jnp.eye(DK, dtype=jnp.float32), (H, DK, DK))
    zeroed = jnp.zeros((H, DK, DK), jnp.float32)
    (matrix, offset), unused = lax.scan(
        fold_block, (identity, zeroed), (keys_end, keys_w, values_w, decay_end)
    )

    def combine(earlier_pair, later_pair):
        return join_pairs(earlier_pair, later_pair)

    prefix = carried_in((matrix, offset), "seq", combine, (identity, zeroed))
    incoming = prefix[1]
    final_state, outputs = lax.scan(advance, incoming, terms)
    core = outputs.transpose(0, 2, 1, 3).reshape(count, H, DK)
    return finish(core, gate_value, norm_gain, count)


def solution(mesh):
    in_specs = (
        P(("rep", "seq"), None),
        P(None, "seq"),
        P(),
        P(),
        P(),
        P(),
        P(),
        P(),
        P(),
        P(),
        P(),
    )
    out_specs = P(("rep", "seq"), None)
    return jax.shard_map(
        per_device, mesh=mesh, in_specs=in_specs, out_specs=out_specs, check_vma=False
    )
```

profile of v0, /device:TPU:1, one launch (start us, length us, event | category | flops | bytes accessed | tf_op | source)
XLA Modules:
  0.0 684.3 jit_solution(2664302093057689382)
XLA Ops:
  10.9 13.1 %fusion.63 = f32[2,16,64,128]{3,1,2,0:T(8,128)S(1)} fusion(f32[2,64,16,128]{3,2,1,0:T(8,128)S(1)} %bitcast.180), kind=kOutput, calls=%fused_computation.87 | output fusion | flops 16515072 | bytes 2097152 | tf_op jit(solution)/shard_map/jit(cumsum)/reduce_window_sum | solution.py:69
  24.4 89.2 %all-gather.6.cloned.1.call-done = bf16[2304,6144]{0,1:T(8,128)(2,1)} async-done(((bf16[2304,192]{0,1:T(8,128)(2,1)}), bf16[2304,6144]{0,1:T(8,128)(2,1)}) %all-gather.6.cloned.1.call-update) | async-done | bytes 28311568 | tf_op jit(solution)/shard_map/all_gather | solution.py:142
  113.6 14.3 %convolution_convert_fusion = bf16[128,6144]{1,0:T(8,128)(2,1)S(1)} fusion(bf16[128,2304]{1,0:T(8,128)(2,1)S(1)} %copy-done, bf16[2304,6144]{0,1:T(8,128)(2,1)} %all-gather.6.cloned.1.call-done), kind=kOutput, calls=%fused_computation.48 | convolution fusion | flops 3624665088 | bytes 30474240 | tf_op jit(solution)/shard_map/dot_general | solution.py:140
  128.6 3.4 collective-permute-start
  139.4 3.3 fusion.57
  142.7 158.7 %custom-call.4 = f32[2,16,1,64,64]{3,4,2,1,0:T(8,128)} custom-call(f32[2,16,1,64,64]{4,3,2,1,0:T(8,128)} %fusion.57), custom_call_target="InvertDiagBlocksLowerTriangular" | custom-call | tf_op jit(solution)/shard_map/jit(_solve_triangular)/vmap(vmap())/triangular_solve | solution.py:81
  303.0 3.0 fusion.48
  309.2 20.1 %while.40 = (s32[]{:T(128)}, f32[16,128,128]{2,1,0:T(8,128)}, f32[16,128,128]{2,1,0:T(8,128)}, f32[2,16,128]{2,1,0:T(8,128)S(1)}, f32[2,16,64,128]{3,2,1,0:T(8,1...) while((s32[]{:T(128)}, f32[16,128,128]{2,1,0:T(8,128)}, ...), condition=%wide.region_3.4_spmd.clone, body=%wide.region_2.3_spmd.clone.sunk | while | flops 1209040896 | bytes 22177956 | solution.py:162
  309.2 3.1 convolution_subtract_fusion.5
  318.6 3.1 convolution_subtract_fusion.5
  332.7 4.8 convolution_select_fusion
  337.5 107.0 %all-gather.8.cloned.1.call-done = f32[512,128,128]{2,1,0:T(8,128)} async-done(((f32[16,128,128]{2,1,0:T(8,128)}), f32[512,128,128]{2,1,0:T(8,128)}) %all-gather.8.cloned.1.call-update) | async-done | bytes 33554448 | tf_op jit(solution)/shard_map/all_gather | solution.py:21
  444.5 115.5 %all-gather.10.cloned.1.call-done = f32[512,128,128]{2,1,0:T(8,128)} async-done(((f32[16,128,128]{2,1,0:T(8,128)}), f32[512,128,128]{2,1,0:T(8,128)}) %all-gather.10.cloned.1.call-update) | async-done | bytes 33554448 | tf_op jit(solution)/shard_map/all_gather | solution.py:21
  559.9 94.0 %while.41 = (s32[]{:T(128)}, f32[16,128,128]{2,1,0:T(8,128)S(1)}, s32[]{:T(128)}, f32[32,16,128,128]{3,2,1,0:T(8,128)}, f32[32,16,128,128]{3,2,1,0:T(8,128)}, /*index=5*/s32[]{:T(128)}, s32[]{:T(128)}) while((s32[]{:T(128)}, f32[16,128,128]{2,1,0:T(8,128)S(1)}, s32[]{:T(128)}, f32[32,16,128,128]{3,2,1,0:T(8,128)}, ...), condition=%wide.region_5.6_spmd.clone, body=%wide.region_4.5_spmd.clone.sunk | while | flops 403701760 | bytes 7342687 | solution.py:31
  560.0 2.8 fusion.141
  563.0 2.8 fusion.141
  565.9 2.8 fusion.141
  571.8 2.8 fusion.141
  574.7 2.8 fusion.141
  577.6 2.8 fusion.141
  580.6 2.8 fusion.141
  583.5 2.8 fusion.141
  653.9 17.0 %while.39 = (s32[]{:T(128)}, f32[16,128,128]{2,1,0:T(8,128)S(1)}, f32[2,16,64,128]{3,2,1,0:T(8,128)}, f32[2,16,128]{2,1,0:T(8,128)S(1)}, f32[2,16,64,128]{3,2,1,...) while((s32[]{:T(128)}, f32[16,128,128]{2,1,0:T(8,128)S(1)}, ...), condition=%wide.region_8.9_spmd, body=%wide.region_7.8_spmd.sunk | while | flops 705429504 | bytes 22571712 | solution.py:171
  674.9 2.9 fusion.47
  (166 shorter events, 125.6 us)
Async XLA Ops:
  6.5 1.5 copy-start
  6.5 107.1 %all-gather.6.cloned.1.call-start = ((), (), s32[]{:S(2)}) async-start(), calls=%async_computation | async-start | bytes 29196288 | tf_op jit(solution)/shard_map/all_gather | solution.py:142
  7.3 437.2 %all-gather.8.cloned.1.call-start = ((), (), s32[]{:S(2)}) async-start(), calls=%async_computation.1 | async-start | bytes 34603008 | tf_op jit(solution)/shard_map/all_gather | solution.py:21
  9.9 14.0 %copy-start.12 = (bf16[2304,16]{0,1:T(8,128)(2,1)S(1)}, bf16[2304,16]{0,1:T(8,128)(2,1)}, u32[]{:S(2)}) copy-start(bf16[2304,16]{0,1:T(8,128)(2,1)} %param.23) | copy-start | bytes 221188
  9.9 14.0 %copy-start.15 = (f32[16]{0:T(128)S(1)}, f32[16]{0:T(128)}, u32[]{:S(2)}) copy-start(f32[16]{0:T(128)} %param.24) | copy-start | bytes 196
  10.0 14.3 %copy-start.11 = (f32[4,6144]{1,0:T(4,128)S(1)}, f32[4,6144]{1,0:T(4,128)}, u32[]{:S(2)}) copy-start(f32[4,6144]{1,0:T(4,128)} %param.19) | copy-start | bytes 294916
  23.9 104.0 %copy-start.5 = (f32[2,16,64,128]{3,1,2,0:T(8,128)}, f32[2,16,64,128]{3,1,2,0:T(8,128)S(1)}, u32[]{:S(2)}) copy-start(f32[2,16,64,128]{3,1,2,0:T(8,128)S(1)} %fusion.63) | copy-start | bytes 3145732
  128.6 4.7 collective-permute-start
  136.0 1.6 copy-start.6
  137.6 1.8 copy-start.13
  137.6 1.8 copy-start.14
  139.4 163.6 %copy-start.4 = (f32[2,16,64,128]{3,1,2,0:T(8,128)}, f32[2,16,64,128]{3,1,2,0:T(8,128)S(1)}, u32[]{:S(2)}) copy-start(f32[2,16,64,128]{3,1,2,0:T(8,128)S(1)} %get-tuple-element.325) | copy-start | bytes 3145732
  301.4 1.7 copy-start.10
  306.1 1.7 copy-start.7
  309.2 20.9 %copy-start.16 = (f32[128]{0:T(128)S(1)}, f32[128]{0:T(128)}, u32[]{:S(2)}) copy-start(f32[128]{0:T(128)} %param.27) | copy-start | bytes 1540
  312.3 4.0 copy-start.1
  321.6 2.6 copy-start.2
  321.6 5.4 copy-start.1
  329.3 230.6 %all-gather.10.cloned.1.call-start = ((), (), s32[]{:S(2)}) async-start(), calls=%async_computation.2 | async-start | bytes 34603008 | tf_op jit(solution)/shard_map/all_gather | solution.py:21
  653.9 4.1 copy-start.3
  653.9 4.1 copy-start.8
  662.4 4.1 copy-start.3
  662.4 4.1 copy-start.8
  671.0 3.9 copy-start.17
  (3 other events, 3.3 us)
Sparse Core Ops, SparseCore 0:
  9.6 103.9 all-gather.5
  329.4 114.9 all-gather.7
  446.7 113.1 all-gather.9
where the time goes:
time: 686 us; the launch traced here: 684 us
  waiting for transfers between devices  314 us (46%)
  other arithmetic  182 us (27%)
  matrix products  155 us (23%)
  local copies, waits for them, and re-layouts  14.4 us (2%)
  between operations  13.5 us (2%)
    all_gather x2, waiting for transfers between devices, carried_in(): everything = jax.tree.map(lambda part: lax.all_gather(part, axis), x)  222 us
    another operation x2, other arithmetic, block_terms(): jax.scipy.linalg.solve_triangular(system, right_side, lower=True, unit_di...  159 us
    dot_general x36, matrix products, matmul(): return jnp.einsum('...de,...ef->...df', left, right, precision=precise)  98.3 us
    all_gather x1, waiting for transfers between devices, per_device(): lax.all_gather(qkv_weight, 'seq', axis=1, tiled=True)  89.2 us
    dot_general x1, matrix products, per_device(): jnp.dot(tokens, lax.all_gather(qkv_weight, 'seq', axis=1, tiled=True), pr...  14.3 us
  transfers between devices with their start and end apart: 4, of which 4 were waited for; matrix products, arithmetic and copies ran while one was open for 4% of the time, Pallas kernels for 0%

commit v1 on v0

--- a/solution.py
+++ b/solution.py
@@ -137,10 +137,17 @@
     norm_gain,
 ):
     count = tokens.shape[0]
+
+    def derive_threads(tile_in, which_axis):
+        return jnp.concatenate(
+            lax.all_to_all(
+                jnp.stack([tile_in for _ in range(lax.axis_size(which_axis))], 0), which_axis, 0, 0
+            ),
+            1,
+        )
+
     mixed = jnp.dot(
-        tokens,
-        lax.all_gather(qkv_weight, "seq", axis=1, tiled=True),
-        preferred_element_type=jnp.float32,
+        tokens, derive_threads(qkv_weight, "seq"), preferred_element_type=jnp.float32
     ).astype(jnp.bfloat16)
     earlier = from_behind(mixed[count - (CONV - 1) :], "seq", 1)
     padded = jnp.concatenate([earlier, mixed], axis=0)

time: 686 us -> 966 us (1.41)
  waiting for transfers between devices: 314 us -> 571 us
  starting transfers between devices: 3.45 us -> 17.7 us
  local copies, waits for them, and re-layouts: 14.4 us -> 24.8 us
    all_to_all x0 -> x1, waiting for transfers between devices: none -> 333 us  [derive_threads(): lax.all_to_all(jnp.stack([tile_in for _ in range(lax.axis_size(which_axis...]
    all_gather x1 -> x0, waiting for transfers between devices: 89.2 us -> none  [per_device(): lax.all_gather(qkv_weight, 'seq', axis=1, tiled=True)]
    ppermute x1, waiting for transfers between devices: 1.1 us -> 13.3 us  [from_behind(): return lax.ppermute(block, axis, route)]
    another operation x0 -> x1, local copies, waits for them, and re-layouts: none -> 10.4 us  [derive_threads(): jnp.stack([tile_in for _ in range(lax.axis_size(which_axis))], 0)]
  transfers between devices with their start and end apart: 4 -> 4, of which waited for: 4 -> 4; matrix products, arithmetic and copies ran while one was open for 4% -> 2% of each run, Pallas kernels for 0% -> 0%
where the time goes in v1:
time: 966 us; the launch traced here: 964 us
  waiting for transfers between devices  571 us (59%)
  other arithmetic  181 us (19%)
  matrix products  154 us (16%)
  local copies, waits for them, and re-layouts  24.8 us (3%)
  starting transfers between devices  17.7 us (2%)
  between operations  13.8 us (1%)
    all_to_all x1, waiting for transfers between devices, derive_threads(): lax.all_to_all(jnp.stack([tile_in for _ in range(lax.axis_size(which_axis...  333 us
    all_gather x2, waiting for transfers between devices, carried_in(): everything = jax.tree.map(lambda part: lax.all_gather(part, axis), x)  224 us
    another operation x2, other arithmetic, block_terms(): jax.scipy.linalg.solve_triangular(system, right_side, lower=True, unit_di...  159 us
    dot_general x36, matrix products, matmul(): return jnp.einsum('...de,...ef->...df', left, right, precision=precise)  98.3 us
  transfers between devices with their start and end apart: 4, of which 4 were waited for; matrix products, arithmetic and copies ran while one was open for 2% of the time, Pallas kernels for 0%

profile of v1, /device:TPU:1, one launch (start us, length us, event | category | flops | bytes accessed | tf_op | source)
XLA Modules:
  0.0 964.0 jit_solution(10977535629629678419)
XLA Ops:
  6.5 10.4 %stack.2 = bf16[32,2304,192]{1,2,0:T(8,128)(2,1)} broadcast(bf16[2304,192]{0,1:T(8,128)(2,1)} %param.18), dimensions={1,2} | broadcast | bytes 29196288 | tf_op jit(solution)/shard_map/stack | solution.py:144
  17.0 9.6 all-to-all-start
  28.4 13.1 %fusion.63 = f32[2,16,64,128]{3,1,2,0:T(8,128)S(1)} fusion(f32[2,64,16,128]{3,2,1,0:T(8,128)S(1)} %bitcast.183), kind=kOutput, calls=%fused_computation.87 | output fusion | flops 16515072 | bytes 2097152 | tf_op jit(solution)/shard_map/jit(cumsum)/reduce_window_sum | solution.py:69
  41.9 333.0 %all-to-all-done = bf16[32,2304,192]{1,2,0:T(8,128)(2,1)} async-done(((bf16[32,2304,192]{1,2,0:T(8,128)(2,1)}), bf16[32,2304,192]{1,2,0:T(8,128)(2,1)}, u32[]{:S(2)}, u32[]{:S(2)}) %all-to-all-start) | async-done | bytes 28311584 | tf_op jit(solution)/shard_map/all_to_all | solution.py:143
  374.9 14.3 %convolution_convert_fusion = bf16[128,6144]{1,0:T(8,128)(2,1)S(1)} fusion(bf16[128,2304]{1,0:T(8,128)(2,1)S(1)} %copy-done, bf16[2304,6144]{0,1:T(8,128)(2,1)} %bitcast.11), kind=kOutput, calls=%fused_computation.48 | convolution fusion | flops 3624665088 | bytes 30474240 | tf_op jit(solution)/shard_map/dot_general | solution.py:149
  389.9 8.0 collective-permute-start
  398.1 13.3 %collective-permute-done = bf16[3,6144]{1,0:T(4,128)(2,1)S(1)} collective-permute-done((bf16[3,6144]{1,0:T(4,128)(2,1)}, bf16[3,6144]{1,0:T(4,128)(2,1)S(1)}, u32[]{:S(2)}, u32[]{:S(2)}) %collective-permute-start) | collective-permute-done | bytes 36896 | tf_op jit(solution)/shard_map/ppermute | solution.py:16
  417.4 3.3 fusion.57
  420.7 158.7 %custom-call.4 = f32[2,16,1,64,64]{3,4,2,1,0:T(8,128)} custom-call(f32[2,16,1,64,64]{4,3,2,1,0:T(8,128)} %fusion.57), custom_call_target="InvertDiagBlocksLowerTriangular" | custom-call | tf_op jit(solution)/shard_map/jit(_solve_triangular)/vmap(vmap())/triangular_solve | solution.py:81
  581.1 3.0 fusion.48
  587.2 20.1 %while.40 = (s32[]{:T(128)}, f32[16,128,128]{2,1,0:T(8,128)}, f32[16,128,128]{2,1,0:T(8,128)}, f32[2,16,128]{2,1,0:T(8,128)S(1)}, f32[2,16,64,128]{3,2,1,0:T(8,1...) while((s32[]{:T(128)}, f32[16,128,128]{2,1,0:T(8,128)}, ...), condition=%wide.region_3.4_spmd.clone, body=%wide.region_2.3_spmd.clone.sunk | while | flops 1209040896 | bytes 22177956 | solution.py:169
  587.2 3.1 convolution_subtract_fusion.5
  596.6 3.1 convolution_subtract_fusion.5
  610.7 4.8 convolution_select_fusion
  615.5 108.3 %all-gather.5.cloned.1.call-done = f32[512,128,128]{2,1,0:T(8,128)} async-done(((f32[16,128,128]{2,1,0:T(8,128)}), f32[512,128,128]{2,1,0:T(8,128)}) %all-gather.5.cloned.1.call-update) | async-done | bytes 33554448 | tf_op jit(solution)/shard_map/all_gather | solution.py:21
  723.8 115.5 %all-gather.7.cloned.1.call-done = f32[512,128,128]{2,1,0:T(8,128)} async-done(((f32[16,128,128]{2,1,0:T(8,128)}), f32[512,128,128]{2,1,0:T(8,128)}) %all-gather.7.cloned.1.call-update) | async-done | bytes 33554448 | tf_op jit(solution)/shard_map/all_gather | solution.py:21
  839.3 94.0 %while.41 = (s32[]{:T(128)}, f32[16,128,128]{2,1,0:T(8,128)S(1)}, s32[]{:T(128)}, f32[32,16,128,128]{3,2,1,0:T(8,128)}, f32[32,16,128,128]{3,2,1,0:T(8,128)}, /*index=5*/s32[]{:T(128)}, s32[]{:T(128)}) while((s32[]{:T(128)}, f32[16,128,128]{2,1,0:T(8,128)S(1)}, s32[]{:T(128)}, f32[32,16,128,128]{3,2,1,0:T(8,128)}, ...), condition=%wide.region_5.6_spmd.clone, body=%wide.region_4.5_spmd.clone.sunk | while | flops 403701760 | bytes 7342687 | solution.py:31
  839.4 2.8 fusion.141
  842.3 2.8 fusion.141
  845.2 2.8 fusion.141
  848.2 2.8 fusion.141
  851.1 2.8 fusion.141
  933.2 17.1 %while.39 = (s32[]{:T(128)}, f32[16,128,128]{2,1,0:T(8,128)S(1)}, f32[2,16,64,128]{3,2,1,0:T(8,128)}, f32[2,16,128]{2,1,0:T(8,128)S(1)}, f32[2,16,64,128]{3,2,1,...) while((s32[]{:T(128)}, f32[16,128,128]{2,1,0:T(8,128)S(1)}, ...), condition=%wide.region_8.9_spmd, body=%wide.region_7.8_spmd.sunk | while | flops 705429504 | bytes 22571712 | solution.py:178
  954.2 2.9 fusion.47
  (172 shorter events, 130.3 us)
Async XLA Ops:
  6.5 20.1 %copy-start = (bf16[128,2304]{1,0:T(8,128)(2,1)S(1)}, bf16[128,2304]{1,0:T(8,128)(2,1)}, u32[]{:S(2)}) copy-start(bf16[128,2304]{1,0:T(8,128)(2,1)} %param.17) | copy-start | bytes 1769476
  17.0 9.7 %copy-start.15 = (f32[2048]{0:T(1024)S(1)}, f32[2048]{0:T(1024)}, u32[]{:S(2)}) copy-start(f32[2048]{0:T(1024)} %param.22) | copy-start | bytes 24580
  17.0 9.7 %copy-start.18 = (bf16[2304,128]{1,0:T(8,128)(2,1)S(1)}, bf16[2304,128]{1,0:T(8,128)(2,1)}, u32[]{:S(2)}) copy-start(bf16[2304,128]{1,0:T(8,128)(2,1)} %param.20) | copy-start | bytes 1769476
  17.0 9.7 %copy-start.20 = (bf16[128,2048]{1,0:T(8,128)(2,1)S(1)}, bf16[128,2048]{1,0:T(8,128)(2,1)}, u32[]{:S(2)}) copy-start(bf16[128,2048]{1,0:T(8,128)(2,1)} %param.21) | copy-start | bytes 1572868
  17.0 357.9 %all-to-all-start = ((bf16[32,2304,192]{1,2,0:T(8,128)(2,1)}), bf16[32,2304,192]{1,2,0:T(8,128)(2,1)}, u32[]{:S(2)}, u32[]{:S(2)}) async-start(bf16[32,2304,192]{1,2,0:T(8,128)(2,1)} %stack.2), calls=%async_computation | async-start | bytes 56623104 | tf_op jit(solution)/shard_map/all_to_all | solution.py:143
  26.6 697.2 %all-gather.5.cloned.1.call-start = ((), (), s32[]{:S(2)}) async-start(), calls=%async_computation.1 | async-start | bytes 34603008 | tf_op jit(solution)/shard_map/all_gather | solution.py:21
  27.4 14.0 %copy-start.12 = (bf16[2304,16]{0,1:T(8,128)(2,1)S(1)}, bf16[2304,16]{0,1:T(8,128)(2,1)}, u32[]{:S(2)}) copy-start(bf16[2304,16]{0,1:T(8,128)(2,1)} %param.23) | copy-start | bytes 221188
  27.4 14.0 %copy-start.16 = (f32[16]{0:T(128)S(1)}, f32[16]{0:T(128)}, u32[]{:S(2)}) copy-start(f32[16]{0:T(128)} %param.24) | copy-start | bytes 196
  27.5 14.3 %copy-start.11 = (f32[4,6144]{1,0:T(4,128)S(1)}, f32[4,6144]{1,0:T(4,128)}, u32[]{:S(2)}) copy-start(f32[4,6144]{1,0:T(4,128)} %param.19) | copy-start | bytes 294916
  41.4 347.8 %copy-start.5 = (f32[2,16,64,128]{3,1,2,0:T(8,128)}, f32[2,16,64,128]{3,1,2,0:T(8,128)S(1)}, u32[]{:S(2)}) copy-start(f32[2,16,64,128]{3,1,2,0:T(8,128)S(1)} %fusion.63) | copy-start | bytes 3145732
  389.9 21.4 %collective-permute-start = (bf16[3,6144]{1,0:T(4,128)(2,1)}, bf16[3,6144]{1,0:T(4,128)(2,1)S(1)}, u32[]{:S(2)}, u32[]{:S(2)}) collective-permute-start(bf16[3,6144]{1,0:T(4,128)(2,1)} %slice.64), channel_id=1, source_target_pairs={{0,4},{4,8},{8,12},{12,16},{16,20},{20,24},{24,28},{28,32},{32,36}... | collective-permute-start | bytes 110600 | tf_op jit(solution)/shard_map/ppermute | solution.py:16
  415.7 1.8 copy-start.13
  415.7 1.8 copy-start.14
  417.4 163.6 %copy-start.4 = (f32[2,16,64,128]{3,1,2,0:T(8,128)}, f32[2,16,64,128]{3,1,2,0:T(8,128)S(1)}, u32[]{:S(2)}) copy-start(f32[2,16,64,128]{3,1,2,0:T(8,128)S(1)} %get-tuple-element.341) | copy-start | bytes 3145732
  587.2 20.9 %copy-start.17 = (f32[128]{0:T(128)S(1)}, f32[128]{0:T(128)}, u32[]{:S(2)}) copy-start(f32[128]{0:T(128)} %param.27) | copy-start | bytes 1540
  590.3 4.0 copy-start.1
  599.6 2.6 copy-start.2
  599.7 5.4 copy-start.1
  607.3 232.0 %all-gather.7.cloned.1.call-start = ((), (), s32[]{:S(2)}) async-start(), calls=%async_computation.2 | async-start | bytes 34603008 | tf_op jit(solution)/shard_map/all_gather | solution.py:21
  933.3 4.1 copy-start.3
  933.3 4.1 copy-start.8
  941.8 4.1 copy-start.3
  941.8 4.1 copy-start.8
  950.3 3.9 copy-start.19
  (6 other events, 8.2 us)
Sparse Core Ops, SparseCore 0:
  607.4 116.3 all-gather.4
  726.1 113.1 all-gather.6
